TPU v7x, 256 devices: a whole 4x4x8 slice. The times are simulated.
256 devices in a mesh: seq: 32 (over z, y), head: 8 (over x, core).
Axes of the slice: x: 4, y: 4, z: 8, core: 2. Of those that a mesh axis runs over, the one named last changes fastest.
Arguments:
- x_in: bfloat16 [4096, 8192], P('seq', 'head'), may hold values from -6 to 6
- z_gate: bfloat16 [4096, 8192], P('seq', 'head'), may hold values from -6 to 6
- b_in: bfloat16 [4096, 2048], P('seq', 'head'), may hold values from -0.75 to 0.75
- c_in: bfloat16 [4096, 2048], P('seq', 'head'), may hold values from -0.75 to 0.75
- log_decay: float32 [4096, 128], P('seq', 'head'), may hold values from 0 to 1.5
- step_size: float32 [4096, 128], P('seq', 'head'), may hold values from 0.3 to 3
- d_skip: float32 [128], P('head'), may hold values from 0.5 to 2
- norm_gain: float32 [8192], P('head'), may hold values from 0.25 to 1.75
- w_out: bfloat16 [8192, 4096], P('head'), may hold values from -0.0625 to 0.0625
- residual: bfloat16 [4096, 4096], P(('seq', 'head')), may hold values from -8 to 8
- final_gain: float32 [4096], replicated, may hold values from 0.25 to 1.75
- vocab: bfloat16 [65536, 4096], P(('seq', 'head')), may hold values from -12 to 12
- targets: int32 [32, 128], P(None, 'head'), may hold values from 0 to 65535
Outputs:
- hidden_out: float32 [4096, 4096], P(('seq', 'head'))
- logprob: float32 [4096], P(('seq', 'head'))
All inputs are finite; a program needn't handle non-finite values.
Results may differ from a plain program's by a relative error of at most 0.0029.
Values may be sent and summed in bfloat16 or wider, within the bound.
No kernel may reach another device: no remote copies, remote signals or barrier semaphores. Data moves between devices by JAX's collectives and lax.ppermute only.
A program may use at most 128 MiB of HBM per device.

v0:
```python
import jax
import jax.numpy as jnp
from jax import lax
from jax.sharding import PartitionSpec as P

SCAN_LANE_NUMBER = 128
HEAD_DIM = 64
STATE = 256
GROUPS = 8
INNER = 8192
epsilon = 1e-05
highest = lax.Precision.HIGHEST


def carried_in(value, axis, combine, identity):
    count, mine = (lax.axis_size(axis), lax.axis_index(axis))
    everything = jax.tree.map(lambda part: lax.all_gather(part, axis), value)
    start = jax.tree.map(
        lambda part, zero: jnp.broadcast_to(jnp.asarray(zero, part.dtype), part.shape),
        value,
        identity,
    )

    def hop(k, before):
        reached = k < mine
        new = combine(before, jax.tree.map(lambda part: part[k], everything))
        return jax.tree.map(lambda a, b: jnp.where(reached, a, b), new, before)

    return lax.fori_loop(0, count, hop, start)


def joined(part, axis, combine):
    gathered = jax.tree.map(lambda a: lax.all_gather(a, axis), part)

    def take(source):
        return jax.tree.map(lambda a: lax.dynamic_index_in_dim(a, source, 0, False), gathered)

    return lax.fori_loop(
        1, lax.axis_size(axis), lambda source, state: combine(state, take(source)), take(0)
    )


def local_terms(inputs, b_rows, c_rows, decays, step_rows, per_group):
    length = inputs.shape[0]
    cumulative = jnp.cumsum(decays, axis=0)
    by_head = cumulative.T
    gaps = by_head[:, None, :] - by_head[:, :, None]
    positions = jnp.arange(length)
    causal = positions[None, :] <= positions[:, None]
    segment_w = jnp.where(causal[None], jnp.exp(jnp.minimum(gaps, 0.0)), 0.0)
    scores = jnp.einsum("tgn,sgn->gts", c_rows, b_rows, precision=highest)
    head_scores = jnp.repeat(scores, per_group, axis=0)
    weights = segment_w * head_scores * step_rows.T[:, None, :]
    within = jnp.einsum("hts,shp->thp", weights, inputs, precision=highest)
    last = cumulative[-1]
    end_weight = jnp.exp(last[None, :] - cumulative) * step_rows
    b_heads = jnp.repeat(b_rows, per_group, axis=1)
    end_state = jnp.einsum(
        "shp,shn->hpn", inputs * end_weight[:, :, None], b_heads, precision=highest
    )
    return (within, cumulative, end_state, jnp.exp(-last))


def carried(c_rows, cumulative, state, per_group):
    c_heads = jnp.repeat(c_rows, per_group, axis=1)
    return jnp.exp(-cumulative)[:, :, None] * jnp.einsum(
        "thn,hpn->thp", c_heads, state, precision=highest
    )


def chain(earlier, later):
    return (earlier[0] * later[0], later[0][:, None, None] * earlier[1] + later[1])


def vocab_fold(token_all, wanted, offset):

    def update(carry, piece, start):
        top, total, picked = carry
        logits = lax.dot_general(
            token_all, piece, (((1,), (1,)), ((), ())), preferred_element_type=jnp.float32
        )
        new_top = jnp.max(logits, axis=1)
        total = total * jnp.exp(top - new_top) + jnp.sum(jnp.exp(logits - new_top[:, None]), axis=1)
        vocab_ids = offset + lax.broadcasted_iota(jnp.int32, (1, piece.shape[0]), 1)
        picked = jnp.sum(jnp.where(vocab_ids == wanted[:, None], logits, 0.0), axis=1)
        return (new_top, total, picked)

    return update


def combine(first, second):
    top = jnp.maximum(first[0], second[0])
    total = first[1] * jnp.exp(first[0] - top) + second[1] * jnp.exp(second[0] - top)
    return (top, total, first[2] + second[2])


def start_triple(count):
    return (
        jnp.full((count,), -jnp.inf, jnp.float32),
        jnp.zeros((count,), jnp.float32),
        jnp.zeros((count,), jnp.float32),
    )


def shards(
    x_in,
    z_gate,
    b_in,
    c_in,
    log_decay,
    step_size,
    d_skip,
    norm_gain,
    w_out,
    residual,
    final_gain,
    vocab,
    targets,
):
    per_group = SCAN_LANE_NUMBER // GROUPS
    length = x_in.shape[0]
    head_count = log_decay.shape[1]
    group_count = b_in.shape[1] // STATE
    inputs = x_in.astype(jnp.float32).reshape(length, head_count, HEAD_DIM)
    b_rows = b_in.astype(jnp.float32).reshape(length, group_count, STATE)
    c_rows = c_in.astype(jnp.float32).reshape(length, group_count, STATE)
    within, cumulative, end_state, decay = local_terms(
        inputs, b_rows, c_rows, log_decay, step_size, per_group
    )
    identity = (jnp.ones_like(decay), jnp.zeros_like(end_state))
    incoming = carried_in((decay, end_state), "seq", chain, identity)
    mixed = (
        within
        + carried(c_rows, cumulative, incoming[1], per_group)
        + d_skip[None, :, None] * inputs
    )
    gated = mixed.reshape(length, head_count * HEAD_DIM) * jax.nn.silu(z_gate.astype(jnp.float32))
    grouped = gated.reshape(length, group_count, INNER // GROUPS)
    scaled = grouped * lax.rsqrt(jnp.mean(grouped * grouped, axis=-1, keepdims=True) + epsilon)
    normed_inner = (scaled.reshape(length, head_count * HEAD_DIM) * norm_gain).astype(jnp.bfloat16)
    rows = length // lax.axis_size("head")
    summed = lax.psum_scatter(
        jnp.dot(normed_inner, w_out, preferred_element_type=jnp.float32),
        "head",
        scatter_dimension=0,
        tiled=True,
    )
    hidden_out = residual.astype(jnp.float32) + summed
    normed = (
        hidden_out
        * lax.rsqrt(jnp.mean(hidden_out * hidden_out, axis=-1, keepdims=True) + epsilon)
        * final_gain
    ).astype(jnp.bfloat16)
    token_all = lax.all_gather(normed, "seq", axis=0, tiled=True)
    wanted = targets.reshape(-1)
    offset = lax.axis_index("seq") * (vocab.shape[0] * lax.axis_size("head"))
    update = vocab_fold(token_all, wanted, offset)
    top, total, picked = update(
        start_triple(token_all.shape[0]),
        lax.all_gather(vocab, "head", axis=0, tiled=True),
        jnp.int32(0),
    )
    top, total, picked = joined((top, total, picked), "seq", combine)
    every = picked - top - jnp.log(total)
    logprob = lax.dynamic_slice_in_dim(every, lax.axis_index("seq") * rows, rows, 0)
    return (hidden_out, logprob)


def solution(mesh):
    return jax.shard_map(
        shards,
        mesh=mesh,
        in_specs=(
            P("seq", "head"),
            P("seq", "head"),
            P("seq", "head"),
            P("seq", "head"),
            P("seq", "head"),
            P("seq", "head"),
            P("head"),
            P("head"),
            P("head", None),
            P(("seq", "head"), None),
            P(),
            P(("seq", "head"), None),
            P(None, "head"),
        ),
        out_specs=(P(("seq", "head"), None), P(("seq", "head"))),
        check_vma=False,
    )
```

profile of v0, /device:TPU:2, one launch (start us, length us, event | category | flops | bytes accessed | tf_op | source)
XLA Modules:
  0.0 679.8 jit_solution(15846469999163818144)
XLA Ops:
  11.1 2.0 fusion.5
  14.2 43.4 %all-gather.3 = f32[32,1,16]{2,1,0:T(1,128)S(1)} all-gather(f32[1,1,16]{2,1,0:T(1,128)S(1)} %get-tuple-element.331), channel_id=1, replica_groups=mesh['seq'=32,'head'=8] {'seq'}, dimensions={0}, use_global_device_ids=true | all-gather | bytes 2112 | tf_op jit(solution)/shard_map/all_gather | solution.py:17
  57.8 1.4 convolution_bitcast_fusion.1
  59.2 190.0 %all-gather.15.cloned.1.call-done = f32[512,64,256]{2,1,0:T(8,128)} async-done(((f32[16,64,256]{2,1,0:T(8,128)}), f32[512,64,256]{2,1,0:T(8,128)}) %all-gather.15.cloned.1.call-update) | async-done | bytes 33554448 | tf_op jit(solution)/shard_map/all_gather | solution.py:17
  249.2 48.2 %while.34 = (s32[]{:T(128)}, f32[16,64,256]{2,1,0:T(8,128)S(1)}, s32[]{:T(128)}, f32[32,16]{1,0:T(8,128)S(1)}, f32[32,16,64,256]{3,2,1,0:T(8,128)}, /*index=5*/s32[]{:T(128)}, s32[]{:T(128)}) while((s32[]{:T(128)}, f32[16,64,256]{2,1,0:T(8,128)S(1)}, s32[]{:T(128)}, f32[32,16]{1,0:T(8,128)S(1)}, f32[32,16,64,256]{3,2,1,0:T(8,128)}, ...), condition=%wide.region_2.3_spmd.clone, body=%wide.region_1.2_spmd.clone.sunk | while | flops 1048580 | bytes 3146025 | solution.py:29
  249.2 1.5 fusion.39
  250.7 1.5 fusion.39
  252.2 1.5 fusion.39
  253.7 1.5 fusion.39
  255.2 1.5 fusion.39
  256.7 1.5 fusion.39
  258.3 1.5 fusion.39
  259.8 1.5 fusion.39
  261.3 1.5 fusion.39
  262.8 1.5 fusion.39
  264.3 1.5 fusion.39
  265.8 1.5 fusion.39
  267.3 1.5 fusion.39
  268.8 1.5 fusion.39
  270.3 1.5 fusion.39
  271.8 1.5 fusion.39
  273.3 1.5 fusion.39
  274.8 1.5 fusion.39
  276.3 1.5 fusion.39
  277.8 1.5 fusion.39
  279.3 1.5 fusion.39
  280.8 1.5 fusion.39
  282.3 1.5 fusion.39
  283.8 1.5 fusion.39
  285.3 1.5 fusion.39
  286.8 1.5 fusion.39
  288.3 1.5 fusion.39
  289.9 1.5 fusion.39
  291.4 1.5 fusion.39
  292.9 1.5 fusion.39
  294.4 1.5 fusion.39
  295.9 1.5 fusion.39
  297.4 2.3 fusion.3
  300.1 6.1 fusion.23
  307.1 29.6 %reduce-scatter.2.cloned.1.call-done = f32[16,4096]{1,0:T(8,128)} async-done(((f32[128,4096]{1,0:T(8,128)}), f32[16,4096]{1,0:T(8,128)}) %reduce-scatter.2.cloned.1.call-update) | async-done | bytes 262160 | tf_op jit(solution)/shard_map/reduce_scatter | solution.py:142
  338.7 89.0 %all-gather.13.cloned.1.call-done = bf16[2048,4096]{1,0:T(8,128)(2,1)} async-done(((bf16[256,4096]{1,0:T(8,128)(2,1)}), bf16[2048,4096]{1,0:T(8,128)(2,1)}) %all-gather.13.cloned.1.call-update) | async-done | bytes 16777232 | tf_op jit(solution)/shard_map/all_gather | solution.py:160
  427.8 85.3 %all-gather.11.cloned.1.call-done = bf16[512,4096]{1,0:T(8,128)(2,1)} async-done(((bf16[16,4096]{1,0:T(8,128)(2,1)}), bf16[512,4096]{1,0:T(8,128)(2,1)}) %all-gather.11.cloned.1.call-update) | async-done | bytes 4194320 | tf_op jit(solution)/shard_map/all_gather | solution.py:154
  513.0 13.3 %fusion.29 = (f32[512]{0:T(512)S(1)}, f32[512,2048]{1,0:T(8,128)S(1)}) fusion(bf16[512,4096]{1,0:T(8,128)(2,1)} %all-gather.11.cloned.1.call-done, bf16[2048,4096]{1,0:T(8,128)(2,1)} %all-gather.13.cloned.1.call-done), kind=kOutput, calls=%fused_computation.60 | convolution fusion | flops 8590983168 | bytes 25167872 | tf_op jit(solution)/shard_map/dot_general | solution.py:79
  526.3 1.2 select_reduce_fusion
  527.5 47.6 %all-gather.5 = f32[32,1,512]{2,1,0:T(1,128)S(1)} all-gather(f32[1,1,512]{2,1,0:T(1,128)S(1)} %bitcast.80), channel_id=1, replica_groups=mesh['seq'=32,'head'=8] {'seq'}, dimensions={0}, use_global_device_ids=true | all-gather | bytes 67584 | tf_op jit(solution)/shard_map/all_gather | solution.py:33
  575.1 47.0 %all-gather.6 = f32[32,1,512]{2,1,0:T(1,128)S(1)} all-gather(f32[1,1,512]{2,1,0:T(1,128)S(1)} %bitcast.78), channel_id=4, replica_groups=mesh['seq'=32,'head'=8] {'seq'}, dimensions={0}, use_global_device_ids=true | all-gather | bytes 67584 | tf_op jit(solution)/shard_map/all_gather | solution.py:33
  622.1 47.6 %all-gather.4 = f32[32,1,512]{2,1,0:T(1,128)S(1)} all-gather(f32[1,1,512]{2,1,0:T(1,128)S(1)} %bitcast.76), channel_id=3, replica_groups=mesh['seq'=32,'head'=8] {'seq'}, dimensions={0}, use_global_device_ids=true | all-gather | bytes 67584 | tf_op jit(solution)/shard_map/all_gather | solution.py:33
  669.7 2.9 while.33
  (216 shorter events, 11.0 us)
Async XLA Ops:
  7.2 50.6 %copy-start.6 = (f32[128,16]{0,1:T(8,128)S(1)}, f32[128,16]{0,1:T(8,128)}, u32[]{:S(2)}) copy-start(f32[128,16]{0,1:T(8,128)} %param.22) | copy-start | bytes 24580
  7.2 50.4 %copy-start.1 = (bf16[128,256]{1,0:T(8,128)(2,1)S(1)}, bf16[128,256]{1,0:T(8,128)(2,1)}, u32[]{:S(2)}) copy-start(bf16[128,256]{1,0:T(8,128)(2,1)} %param.19) | copy-start | bytes 196612
  7.2 50.4 %copy-start.2 = (bf16[128,256]{1,0:T(8,128)(2,1)S(1)}, bf16[128,256]{1,0:T(8,128)(2,1)}, u32[]{:S(2)}) copy-start(bf16[128,256]{1,0:T(8,128)(2,1)} %param.20) | copy-start | bytes 196612
  7.2 242.0 %all-gather.15.cloned.1.call-start = ((), (), s32[]{:S(2)}) async-start(), calls=%async_computation.4 | async-start | bytes 34603008 | tf_op jit(solution)/shard_map/all_gather | solution.py:17
  13.1 323.5 %reduce-scatter.2.cloned.1.call-start = ((), (), s32[]{:S(2)}) async-start(), calls=%async_computation.1 | async-start | bytes 2359296 | tf_op jit(solution)/shard_map/reduce_scatter | solution.py:142
  249.2 48.2 %copy-start.8 = (f32[16]{0:T(128)S(1)}, f32[16]{0:T(128)}, u32[]{:S(2)}) copy-start(f32[16]{0:T(128)} %param.23) | copy-start | bytes 196
  249.2 50.7 %copy-start.3 = (bf16[128,1024]{1,0:T(8,128)(2,1)S(1)}, bf16[128,1024]{1,0:T(8,128)(2,1)}, u32[]{:S(2)}) copy-start(bf16[128,1024]{1,0:T(8,128)(2,1)} %param.18) | copy-start | bytes 786436
  297.3 2.8 copy-start.9
  306.3 30.4 %copy-start.4 = (bf16[16,4096]{1,0:T(8,128)(2,1)S(1)}, bf16[16,4096]{1,0:T(8,128)(2,1)}, u32[]{:S(2)}) copy-start(bf16[16,4096]{1,0:T(8,128)(2,1)} %param.26) | copy-start | bytes 393220
  306.3 31.5 %copy-start.5 = (f32[4096]{0:T(1024)S(1)}, f32[4096]{0:T(1024)}, u32[]{:S(2)}) copy-start(f32[4096]{0:T(1024)} %param.27) | copy-start | bytes 49156
  306.3 32.3 %copy-start.7 = (s32[32,16]{0,1:T(8,128)S(1)}, s32[32,16]{0,1:T(8,128)}, u32[]{:S(2)}) copy-start(s32[32,16]{0,1:T(8,128)} %param.29) | copy-start | bytes 6148
  306.3 121.5 %all-gather.13.cloned.1.call-start = ((), (), s32[]{:S(2)}) async-start(), calls=%async_computation.3 | async-start | bytes 18874368 | tf_op jit(solution)/shard_map/all_gather | solution.py:160
  307.0 206.0 %all-gather.11.cloned.1.call-start = ((), (), s32[]{:S(2)}) async-start(), calls=%async_computation.2 | async-start | bytes 4325376 | tf_op jit(solution)/shard_map/all_gather | solution.py:154
  337.8 188.5 %copy-start = (f32[16,4096]{1,0:T(8,128)}, f32[16,4096]{1,0:T(8,128)S(1)}, u32[]{:S(2)}) copy-start(f32[16,4096]{1,0:T(8,128)S(1)} %get-tuple-element.325) | copy-start | bytes 786436
Sparse Core Ops, SparseCore 0:
  13.2 235.8 all-gather.14
  306.4 30.1 reduce-scatter.1
  338.5 89.1 all-gather.12
  430.2 82.7 all-gather.10
where the time goes:
time: 681 us; the launch traced here: 680 us
  waiting for transfers between devices  395 us (58%)
  blocking collectives  186 us (27%)
  other arithmetic  53.1 us (8%)
  matrix products  25.1 us (4%)
  between operations  14 us (2%)
    all_gather x1, waiting for transfers between devices, carried_in(): everything = jax.tree.map(lambda part: lax.all_gather(part, axis), value)  190 us
    all_gather x3, blocking collectives, joined(): gathered = jax.tree.map(lambda a: lax.all_gather(a, axis), part)  142 us
    all_gather x1, waiting for transfers between devices, shards(): lax.all_gather(vocab, 'head', axis=0, tiled=True)  89 us
    all_gather x1, waiting for transfers between devices, shards(): token_all = lax.all_gather(normed, 'seq', axis=0, tiled=True)  85.3 us
    select_n x32, other arithmetic, hop(): return jax.tree.map(lambda a, b: jnp.where(reached, a, b), new, before)  46.9 us
    all_gather x1, blocking collectives, carried_in(): everything = jax.tree.map(lambda part: lax.all_gather(part, axis), value)  43.4 us
    reduce_scatter x1, waiting for transfers between devices, shards(): lax.psum_scatter(jnp.dot(normed_inner, w_out, preferred_element_type=jnp....  29.6 us
  transfers between devices with their start and end apart: 4, of which 4 were waited for; matrix products, arithmetic and copies ran while one was open for 1% of the time, Pallas kernels for 0%

commit v1 on v0

--- a/solution.py
+++ b/solution.py
@@ -151,7 +151,8 @@
         * lax.rsqrt(jnp.mean(hidden_out * hidden_out, axis=-1, keepdims=True) + epsilon)
         * final_gain
     ).astype(jnp.bfloat16)
-    token_all = lax.all_gather(normed, "seq", axis=0, tiled=True)
+    repeated = jnp.stack([normed] * lax.axis_size("seq"))
+    token_all = jnp.concatenate(lax.all_to_all(repeated, "seq", 0, 0), axis=0)
     wanted = targets.reshape(-1)
     offset = lax.axis_index("seq") * (vocab.shape[0] * lax.axis_size("head"))
     update = vocab_fold(token_all, wanted, offset)

time: 681 us -> 619 us (0.909)
  waiting for transfers between devices: 395 us -> 314 us
  starting transfers between devices: 0.16 us -> 10.2 us
    all_gather x1 -> x0, waiting for transfers between devices: 85.3 us -> none  [shards(): token_all = lax.all_gather(normed, 'seq', axis=0, tiled=True)]
    all_to_all x0 -> x1, waiting for transfers between devices: none -> 16.9 us  [shards(): token_all = jnp.concatenate(lax.all_to_all(repeated, 'seq', 0, 0), axis=0)]
    all_gather x1, waiting for transfers between devices: 89 us -> 77 us  [shards(): lax.all_gather(vocab, 'head', axis=0, tiled=True)]
    all_to_all x0 -> x1, starting transfers between devices: none -> 10 us  [shards(): token_all = jnp.concatenate(lax.all_to_all(repeated, 'seq', 0, 0), axis=0)]
where the time goes in v1:
time: 619 us; the launch traced here: 614 us
  waiting for transfers between devices  314 us (51%)
  blocking collectives  188 us (30%)
  other arithmetic  52.4 us (8%)
  matrix products  25.1 us (4%)
  between operations  14 us (2%)
  starting transfers between devices  10.2 us (2%)
  local copies, waits for them, and re-layouts  7.5 us (1%)
    all_gather x1, waiting for transfers between devices, carried_in(): everything = jax.tree.map(lambda part: lax.all_gather(part, axis), value)  190 us
    all_gather x3, blocking collectives, joined(): gathered = jax.tree.map(lambda a: lax.all_gather(a, axis), part)  144 us
    all_gather x1, waiting for transfers between devices, shards(): lax.all_gather(vocab, 'head', axis=0, tiled=True)  77 us
    select_n x32, other arithmetic, hop(): return jax.tree.map(lambda a, b: jnp.where(reached, a, b), new, before)  46.9 us
    all_gather x1, blocking collectives, carried_in(): everything = jax.tree.map(lambda part: lax.all_gather(part, axis), value)  43.4 us
    reduce_scatter x1, waiting for transfers between devices, shards(): lax.psum_scatter(jnp.dot(normed_inner, w_out, preferred_element_type=jnp....  29.7 us
    all_to_all x1, waiting for transfers between devices, shards(): token_all = jnp.concatenate(lax.all_to_all(repeated, 'seq', 0, 0), axis=0)  16.9 us
    dot_general x1, matrix products, update(): lax.dot_general(token_all, piece, (((1,), (1,)), ((), ())), preferred_ele...  13.3 us
  transfers between devices with their start and end apart: 4, of which 4 were waited for; matrix products, arithmetic and copies ran while one was open for 1% of the time, Pallas kernels for 0%

profile of v1, /device:TPU:2, one launch (start us, length us, event | category | flops | bytes accessed | tf_op | source)
XLA Modules:
  0.0 613.6 jit_solution(16819321133181599598)
XLA Ops:
  11.1 2.0 fusion.5
  14.2 43.4 %all-gather.3 = f32[32,1,16]{2,1,0:T(1,128)S(1)} all-gather(f32[1,1,16]{2,1,0:T(1,128)S(1)} %get-tuple-element.331), channel_id=1, replica_groups=mesh['seq'=32,'head'=8] {'seq'}, dimensions={0}, use_global_device_ids=true | all-gather | bytes 2112 | tf_op jit(solution)/shard_map/all_gather | solution.py:17
  59.1 190.0 %all-gather.12.cloned.1.call-done = f32[512,64,256]{2,1,0:T(8,128)} async-done(((f32[16,64,256]{2,1,0:T(8,128)}), f32[512,64,256]{2,1,0:T(8,128)}) %all-gather.12.cloned.1.call-update) | async-done | bytes 33554448 | tf_op jit(solution)/shard_map/all_gather | solution.py:17
  249.2 48.2 %while.34 = (s32[]{:T(128)}, f32[16,64,256]{2,1,0:T(8,128)S(1)}, s32[]{:T(128)}, f32[32,16]{1,0:T(8,128)S(1)}, f32[32,16,64,256]{3,2,1,0:T(8,128)}, /*index=5*/s32[]{:T(128)}, s32[]{:T(128)}) while((s32[]{:T(128)}, f32[16,64,256]{2,1,0:T(8,128)S(1)}, s32[]{:T(128)}, f32[32,16]{1,0:T(8,128)S(1)}, f32[32,16,64,256]{3,2,1,0:T(8,128)}, ...), condition=%wide.region_2.3_spmd.clone, body=%wide.region_1.2_spmd.clone.sunk | while | flops 1048580 | bytes 3146025 | solution.py:29
  249.2 1.5 fusion.39
  250.7 1.5 fusion.39
  252.2 1.5 fusion.39
  253.7 1.5 fusion.39
  255.2 1.5 fusion.39
  256.7 1.5 fusion.39
  258.2 1.5 fusion.39
  259.7 1.5 fusion.39
  261.2 1.5 fusion.39
  262.8 1.5 fusion.39
  264.3 1.5 fusion.39
  265.8 1.5 fusion.39
  267.3 1.5 fusion.39
  268.8 1.5 fusion.39
  270.3 1.5 fusion.39
  271.8 1.5 fusion.39
  273.3 1.5 fusion.39
  274.8 1.5 fusion.39
  276.3 1.5 fusion.39
  277.8 1.5 fusion.39
  279.3 1.5 fusion.39
  280.8 1.5 fusion.39
  282.3 1.5 fusion.39
  283.8 1.5 fusion.39
  285.3 1.5 fusion.39
  286.8 1.5 fusion.39
  288.3 1.5 fusion.39
  289.8 1.5 fusion.39
  291.3 1.5 fusion.39
  292.8 1.5 fusion.39
  294.4 1.5 fusion.39
  295.9 1.5 fusion.39
  297.4 2.3 fusion.3
  300.1 6.1 fusion.23
  307.0 29.7 %reduce-scatter.2.cloned.1.call-done = f32[16,4096]{1,0:T(8,128)} async-done(((f32[128,4096]{1,0:T(8,128)}), f32[16,4096]{1,0:T(8,128)}) %reduce-scatter.2.cloned.1.call-update) | async-done | bytes 262160 | tf_op jit(solution)/shard_map/reduce_scatter | solution.py:142
  337.9 2.5 stack.2
  340.4 10.0 %all-to-all-start = ((bf16[32,16,4096]{2,1,0:T(8,128)(2,1)}), bf16[32,16,4096]{2,1,0:T(8,128)(2,1)}, u32[]{:S(2)}, u32[]{:S(2)}) async-start(bf16[32,16,4096]{2,1,0:T(8,128)(2,1)} %stack.2), calls=%async_computation.1 | async-start | bytes 8388608 | tf_op jit(solution)/shard_map/all_to_all | solution.py:155
  350.7 77.0 %all-gather.10.cloned.1.call-done = bf16[2048,4096]{1,0:T(8,128)(2,1)} async-done(((bf16[256,4096]{1,0:T(8,128)(2,1)}), bf16[2048,4096]{1,0:T(8,128)(2,1)}) %all-gather.10.cloned.1.call-update) | async-done | bytes 16777232 | tf_op jit(solution)/shard_map/all_gather | solution.py:161
  427.7 16.9 %all-to-all-done = bf16[32,16,4096]{2,1,0:T(8,128)(2,1)} async-done(((bf16[32,16,4096]{2,1,0:T(8,128)(2,1)}), bf16[32,16,4096]{2,1,0:T(8,128)(2,1)}, u32[]{:S(2)}, u32[]{:S(2)}) %all-to-all-start) | async-done | bytes 4194336 | tf_op jit(solution)/shard_map/all_to_all | solution.py:155
  444.6 13.3 %fusion.29 = (f32[512]{0:T(512)S(1)}, f32[512,2048]{1,0:T(8,128)S(1)}) fusion(bf16[512,4096]{1,0:T(8,128)(2,1)} %bitcast.13, bf16[2048,4096]{1,0:T(8,128)(2,1)} %all-gather.10.cloned.1.call-done), kind=kOutput, calls=%fused_computation.60 | convolution fusion | flops 8590983168 | bytes 25167872 | tf_op jit(solution)/shard_map/dot_general | solution.py:79
  459.0 49.9 %all-gather.5 = f32[32,1,512]{2,1,0:T(1,128)S(1)} all-gather(f32[1,1,512]{2,1,0:T(1,128)S(1)} %bitcast.81), channel_id=1, replica_groups=mesh['seq'=32,'head'=8] {'seq'}, dimensions={0}, use_global_device_ids=true | all-gather | bytes 67584 | tf_op jit(solution)/shard_map/all_gather | solution.py:33
  508.9 45.7 %all-gather.6 = f32[32,1,512]{2,1,0:T(1,128)S(1)} all-gather(f32[1,1,512]{2,1,0:T(1,128)S(1)} %bitcast.79), channel_id=4, replica_groups=mesh['seq'=32,'head'=8] {'seq'}, dimensions={0}, use_global_device_ids=true | all-gather | bytes 67584 | tf_op jit(solution)/shard_map/all_gather | solution.py:33
  554.7 48.9 %all-gather.4 = f32[32,1,512]{2,1,0:T(1,128)S(1)} all-gather(f32[1,1,512]{2,1,0:T(1,128)S(1)} %bitcast.77), channel_id=3, replica_groups=mesh['seq'=32,'head'=8] {'seq'}, dimensions={0}, use_global_device_ids=true | all-gather | bytes 67584 | tf_op jit(solution)/shard_map/all_gather | solution.py:33
  603.6 2.9 while.33
  (216 shorter events, 12.9 us)
Async XLA Ops:
  7.2 50.6 %copy-start.6 = (f32[128,16]{0,1:T(8,128)S(1)}, f32[128,16]{0,1:T(8,128)}, u32[]{:S(2)}) copy-start(f32[128,16]{0,1:T(8,128)} %param.22) | copy-start | bytes 24580
  7.2 50.4 %copy-start.1 = (bf16[128,256]{1,0:T(8,128)(2,1)S(1)}, bf16[128,256]{1,0:T(8,128)(2,1)}, u32[]{:S(2)}) copy-start(bf16[128,256]{1,0:T(8,128)(2,1)} %param.19) | copy-start | bytes 196612
  7.2 50.4 %copy-start.2 = (bf16[128,256]{1,0:T(8,128)(2,1)S(1)}, bf16[128,256]{1,0:T(8,128)(2,1)}, u32[]{:S(2)}) copy-start(bf16[128,256]{1,0:T(8,128)(2,1)} %param.20) | copy-start | bytes 196612
  7.2 241.9 %all-gather.12.cloned.1.call-start = ((), (), s32[]{:S(2)}) async-start(), calls=%async_computation.4 | async-start | bytes 34603008 | tf_op jit(solution)/shard_map/all_gather | solution.py:17
  13.1 323.6 %reduce-scatter.2.cloned.1.call-start = ((), (), s32[]{:S(2)}) async-start(), calls=%async_computation.2 | async-start | bytes 2359296 | tf_op jit(solution)/shard_map/reduce_scatter | solution.py:142
  249.1 48.2 %copy-start.8 = (f32[16]{0:T(128)S(1)}, f32[16]{0:T(128)}, u32[]{:S(2)}) copy-start(f32[16]{0:T(128)} %param.23) | copy-start | bytes 196
  249.2 50.7 %copy-start.3 = (bf16[128,1024]{1,0:T(8,128)(2,1)S(1)}, bf16[128,1024]{1,0:T(8,128)(2,1)}, u32[]{:S(2)}) copy-start(bf16[128,1024]{1,0:T(8,128)(2,1)} %param.18) | copy-start | bytes 786436
  297.3 2.8 copy-start.9
  306.2 30.5 %copy-start.4 = (bf16[16,4096]{1,0:T(8,128)(2,1)S(1)}, bf16[16,4096]{1,0:T(8,128)(2,1)}, u32[]{:S(2)}) copy-start(bf16[16,4096]{1,0:T(8,128)(2,1)} %param.26) | copy-start | bytes 393220
  306.2 31.6 %copy-start.5 = (f32[4096]{0:T(1024)S(1)}, f32[4096]{0:T(1024)}, u32[]{:S(2)}) copy-start(f32[4096]{0:T(1024)} %param.27) | copy-start | bytes 49156
  306.3 121.4 %all-gather.10.cloned.1.call-start = ((), (), s32[]{:S(2)}) async-start(), calls=%async_computation.3 | async-start | bytes 18874368 | tf_op jit(solution)/shard_map/all_gather | solution.py:161
  337.8 2.6 copy-start
  340.4 10.1 %copy-start.7 = (s32[32,16]{0,1:T(8,128)S(1)}, s32[32,16]{0,1:T(8,128)}, u32[]{:S(2)}) copy-start(s32[32,16]{0,1:T(8,128)} %param.29) | copy-start | bytes 6148
  340.4 104.1 %all-to-all-start = ((bf16[32,16,4096]{2,1,0:T(8,128)(2,1)}), bf16[32,16,4096]{2,1,0:T(8,128)(2,1)}, u32[]{:S(2)}, u32[]{:S(2)}) async-start(bf16[32,16,4096]{2,1,0:T(8,128)(2,1)} %stack.2), calls=%async_computation.1 | async-start | bytes 8388608 | tf_op jit(solution)/shard_map/all_to_all | solution.py:155
Sparse Core Ops, SparseCore 0:
  13.2 235.8 all-gather.11
  306.4 30.2 reduce-scatter.1
  338.6 89.0 all-gather.9
